TPU v7x, 512 devices: a whole 4x8x8 slice. The times are simulated.
512 devices in a mesh: narrow: 16 (over z, core), wide: 32 (over x, y).
Axes of the slice: x: 4, y: 8, z: 8, core: 2. Of those that a mesh axis runs over, the one named last changes fastest.
Arguments:
- field: float32 [128, 512, 1024], P('narrow', 'wide'), may hold values from -12 to 12
- start_block: float32 [1024, 128], replicated, may hold values from -6 to 6
Outputs:
- mode2_gram: float32 [128, 128], P('narrow', 'wide')
All inputs are finite; a program needn't handle non-finite values.
Results may differ from a plain program's by a relative error of at most 0.0001.
Values sent between devices are 32-bit elements; how exact they have to be, the bound alone decides.
A program may use at most 64 MiB of HBM per device.

v0:
```python
import jax
import jax.numpy as jnp
from jax import lax
from jax.sharding import PartitionSpec as P

RANK = 128
B3 = 16
ITERS = 4


def orthonormal(vectors):
    inner_gram = jnp.dot(vectors.T, vectors, precision=lax.Precision.HIGHEST)
    factor = jnp.linalg.cholesky(inner_gram)
    return jax.scipy.linalg.solve_triangular(factor, vectors.T, lower=True).T


def transposed_product(left, right):
    return lax.dot_general(left, right, (((0,), (0,)), ((), ())), precision=lax.Precision.HIGHEST)


def shards(field, start_block):
    cells_two, cells_three, order_one = field.shape
    unfolded = field.reshape(cells_two * cells_three, order_one)
    subspace = orthonormal(start_block)
    gram_local = transposed_product(unfolded, unfolded)
    gram_whole = lax.psum(gram_local, ("narrow", "wide"))
    for sweep_index in range(ITERS):
        subspace = orthonormal(jnp.dot(gram_whole, subspace, precision=lax.Precision.HIGHEST))
    core_cells = jnp.dot(unfolded, subspace, precision=lax.Precision.HIGHEST)
    core_block = core_cells.reshape(cells_two, cells_three, subspace.shape[1])
    regrouped = lax.all_to_all(core_block, "narrow", split_axis=2, concat_axis=0, tiled=True)
    merged = regrouped.reshape(regrouped.shape[0], regrouped.shape[1] * regrouped.shape[2])
    gram_part = jnp.dot(merged, merged.T, precision=lax.Precision.HIGHEST)
    sectioned = lax.psum_scatter(gram_part, "narrow", scatter_dimension=0, tiled=True)
    finished = lax.psum_scatter(sectioned, "wide", scatter_dimension=1, tiled=True)
    return finished / (RANK * B3 * lax.axis_size("wide"))


def solution(mesh):
    return jax.shard_map(
        shards,
        mesh=mesh,
        in_specs=(P("narrow", "wide", None), P()),
        out_specs=P("narrow", "wide"),
        check_vma=False,
    )
```

profile of v0, /device:TPU:64, one launch (start us, length us, event | category | flops | bytes accessed | tf_op | source)
XLA Modules:
  0.0 623.6 jit_solution(12508605151711638905)
XLA Ops:
  6.5 1.0 copy-done
  7.6 5.1 convolution_bitcast_fusion
  12.7 1.0 copy-done.1
  13.7 1.0 fusion.33
  14.8 11.7 %cholesky.89 = f32[128,128]{1,0:T(8,128)S(1)} custom-call(f32[128,128]{1,0:T(8,128)S(1)} %fusion.24), custom_call_target="Cholesky" | custom-call | tf_op jit(solution)/shard_map/jit(cholesky)/cholesky | solution.py:13
  27.2 0.7 fusion.10
  27.9 9.8 %custom-call.9 = f32[1,128,128]{1,2,0:T(8,128)S(1)} custom-call(f32[1,128,128]{2,1,0:T(8,128)S(1)} %fusion.10), custom_call_target="InvertDiagBlocksLowerTriangular" | custom-call | tf_op jit(solution)/shard_map/jit(_solve_triangular)/triangular_solve | solution.py:14
  38.3 263.7 %all-reduce.5.cloned.1.call-done = f32[1024,1024]{1,0:T(8,128)} async-done(((f32[1024,1024]{1,0:T(8,128)}), f32[1024,1024]{1,0:T(8,128)}) %all-reduce.5.cloned.1.call-update) | async-done | bytes 4194320 | tf_op jit(solution)/shard_map/psum | solution.py:26
  302.0 5.4 fusion.34
  307.3 1.0 fusion.35
  308.5 11.7 %cholesky.100 = f32[128,128]{1,0:T(8,128)S(1)} custom-call(f32[128,128]{1,0:T(8,128)S(1)} %fusion.22), custom_call_target="Cholesky" | custom-call | tf_op jit(solution)/shard_map/jit(cholesky)/cholesky | solution.py:13
  321.5 9.8 %custom-call.10 = f32[1,128,128]{1,2,0:T(8,128)S(1)} custom-call(f32[1,128,128]{2,1,0:T(8,128)S(1)} %fusion.11), custom_call_target="InvertDiagBlocksLowerTriangular" | custom-call | tf_op jit(solution)/shard_map/jit(_solve_triangular)/triangular_solve | solution.py:14
  332.0 5.4 fusion.36
  337.4 1.0 fusion.37
  338.6 11.7 %cholesky.111 = f32[128,128]{1,0:T(8,128)S(1)} custom-call(f32[128,128]{1,0:T(8,128)S(1)} %fusion.20), custom_call_target="Cholesky" | custom-call | tf_op jit(solution)/shard_map/jit(cholesky)/cholesky | solution.py:13
  351.6 9.8 %custom-call.11 = f32[1,128,128]{1,2,0:T(8,128)S(1)} custom-call(f32[1,128,128]{2,1,0:T(8,128)S(1)} %fusion.12), custom_call_target="InvertDiagBlocksLowerTriangular" | custom-call | tf_op jit(solution)/shard_map/jit(_solve_triangular)/triangular_solve | solution.py:14
  362.1 5.6 fusion.38
  367.7 1.0 fusion.39
  368.8 11.7 %cholesky.122 = f32[128,128]{1,0:T(8,128)S(1)} custom-call(f32[128,128]{1,0:T(8,128)S(1)} %fusion.18), custom_call_target="Cholesky" | custom-call | tf_op jit(solution)/shard_map/jit(cholesky)/cholesky | solution.py:13
  381.9 9.8 %custom-call.12 = f32[1,128,128]{1,2,0:T(8,128)S(1)} custom-call(f32[1,128,128]{2,1,0:T(8,128)S(1)} %fusion.13), custom_call_target="InvertDiagBlocksLowerTriangular" | custom-call | tf_op jit(solution)/shard_map/jit(_solve_triangular)/triangular_solve | solution.py:14
  392.4 5.4 fusion.40
  397.8 1.0 fusion.41
  398.9 11.7 %cholesky.133 = f32[128,128]{1,0:T(8,128)S(1)} custom-call(f32[128,128]{1,0:T(8,128)S(1)} %fusion.16), custom_call_target="Cholesky" | custom-call | tf_op jit(solution)/shard_map/jit(cholesky)/cholesky | solution.py:13
  411.9 9.8 %custom-call.13 = f32[1,128,128]{1,2,0:T(8,128)S(1)} custom-call(f32[1,128,128]{2,1,0:T(8,128)S(1)} %fusion.14), custom_call_target="InvertDiagBlocksLowerTriangular" | custom-call | tf_op jit(solution)/shard_map/jit(_solve_triangular)/triangular_solve | solution.py:14
  423.5 13.1 %all_to_all.15 = f32[16,1,1024]{2,1,0:T(1,128)S(1)} all-to-all(f32[16,1,1024]{2,1,0:T(1,128)S(1)} %reshape.26), channel_id=1, replica_groups=mesh['narrow'=16,'wide'=32] {'narrow'}, dimensions={0} | all-to-all | bytes 131072 | tf_op jit(solution)/shard_map/all_to_all | solution.py:31
  437.1 0.8 reduce.4
  439.0 0.9 fusion.43
  439.9 1.3 dynamic-slice
  441.1 1.3 dynamic-slice.2
  443.6 97.0 %all-reduce.7.cloned.1.call-done = f32[128,128]{1,0:T(8,128)} async-done(((f32[128,128]{1,0:T(8,128)}), f32[128,128]{1,0:T(8,128)}) %all-reduce.7.cloned.1.call-update) | async-done | bytes 65552
  540.7 0.7 constant_dynamic-slice_fusion
  541.3 74.5 %all-reduce.1 = f32[8,128]{1,0:T(8,128)S(1)} all-reduce(f32[8,128]{1,0:T(8,128)S(1)} %constant_dynamic-slice_fusion), channel_id=3, replica_groups=mesh['narrow'=16,'wide'=32] {'wide'}, use_global_device_ids=true, to_apply=%region_4.7.clone | all-reduce | flops 1024 | bytes 8192
  (44 shorter events, 13.2 us)
Async XLA Ops:
  6.5 1.0 copy-start
  6.5 295.4 %all-reduce.5.cloned.1.call-start = ((), (), s32[]{:S(2)}) async-start(), calls=%async_computation.1 | async-start | bytes 8388608 | tf_op jit(solution)/shard_map/psum | solution.py:26
  12.6 1.0 copy-start.1
  12.7 528.0 %all-reduce.7.cloned.1.call-start = ((), (), s32[]{:S(2)}) async-start(), calls=%async_computation.2 | async-start | bytes 131072
Sparse Core Ops, SparseCore 0:
  12.8 289.1 all-reduce.4
  440.0 100.6 all-reduce.6
where the time goes:
time: 631 us; the launch traced here: 624 us
  waiting for transfers between devices  361 us (57%)
  other arithmetic  115 us (18%)
  blocking collectives  87.6 us (14%)
  matrix products  36.6 us (6%)
  between operations  15.1 us (2%)
  local copies, waits for them, and re-layouts  8.36 us (1%)
    psum x1, waiting for transfers between devices, shards(): gram_whole = lax.psum(gram_local, ('narrow', 'wide'))  264 us
    unnamed x3, waiting for transfers between devices  97.1 us
    unnamed x1, blocking collectives  74.5 us
    another operation x15, other arithmetic, orthonormal(): factor = jnp.linalg.cholesky(inner_gram)  61.9 us
    another operation x10, other arithmetic, orthonormal(): return jax.scipy.linalg.solve_triangular(factor, vectors.T, lower=True).T  52.3 us
    dot_general x4, matrix products, shards(): jnp.dot(gram_whole, subspace, precision=lax.Precision.HIGHEST)  21.8 us
    all_to_all x1, blocking collectives, shards(): lax.all_to_all(core_block, 'narrow', split_axis=2, concat_axis=0, tiled=T...  13.1 us
  transfers between devices with their start and end apart: 2, of which 2 were waited for; matrix products, arithmetic and copies ran while one was open for 4% of the time, Pallas kernels for 0%

commit v1 on v0

v1 whole, which is shorter than its diff:
```python
import jax
import jax.numpy as jnp
from jax import lax
from jax.experimental import pallas as pl
from jax.experimental.pallas import tpu as pltpu
from jax.sharding import PartitionSpec as P

RANK = 128
B3 = 16
ITERS = 4
ROWS = 8
LANES = 128
HIGHEST = lax.Precision.HIGHEST


def lane_copy(block, lane):
    return jnp.broadcast_to(block[:, lane:lane + 1], (ROWS, LANES))


def row_copy(block, row):
    return jnp.broadcast_to(block[row:row + 1, :], (ROWS, LANES))


def tree_sum(terms):
    terms = list(terms)
    while len(terms) > 1:
        terms = [sum(terms[i:i + 2][1:], terms[i]) for i in range(0, len(terms), 2)]
    return terms[0]


def inverse_factor(gram):
    row = lax.broadcasted_iota(jnp.int32, (ROWS, LANES), 0)
    lane = lax.broadcasted_iota(jnp.int32, (ROWS, LANES), 1)
    panels = RANK // ROWS
    left = [gram[ROWS * p:ROWS * (p + 1), :] for p in range(panels)]
    right = [jnp.where(lane == row + ROWS * p, 1.0, 0.0) for p in range(panels)]
    finished = []
    for p in range(panels):
        diag = [lane_copy(left[p], ROWS * p + c) for c in range(ROWS)]
        scaled = [jnp.zeros((ROWS, LANES), jnp.float32) for _ in range(ROWS)]
        for j in range(ROWS):
            pivot = row_copy(diag[j], j)
            inverse = 1.0 / pivot
            root = lax.rsqrt(pivot)
            at_pivot = row == j
            for c in range(j):
                scaled[c] = jnp.where(at_pivot, diag[c] * root, scaled[c])
            scaled[j] = jnp.where(at_pivot, root, scaled[j])
            column = diag[j]
            for c in range(ROWS):
                if c != j:
                    across = row_copy(diag[c], j) * inverse
                    diag[c] = jnp.where(at_pivot, across, diag[c] - column * across)
            diag[j] = jnp.where(at_pivot, inverse, -column * inverse)
        solved_left = tree_sum(diag[c] * row_copy(left[p], c) for c in range(ROWS))
        solved_right = tree_sum(diag[c] * row_copy(right[p], c) for c in range(ROWS))
        finished.append(tree_sum(scaled[c] * row_copy(right[p], c) for c in range(ROWS)))
        left_rows = [row_copy(solved_left, c) for c in range(ROWS)]
        right_rows = [row_copy(solved_right, c) for c in range(ROWS)]
        for q in range(p + 1, panels):
            factors = [lane_copy(left[q], ROWS * p + c) for c in range(ROWS)]
            left[q] = left[q] - tree_sum(factors[c] * left_rows[c] for c in range(ROWS))
            right[q] = right[q] - tree_sum(factors[c] * right_rows[c] for c in range(ROWS))
    return jnp.concatenate(finished, axis=0)


def product(left, right):
    return lax.dot_general(left, right, (((1,), (0,)), ((), ())), precision=HIGHEST,
                           preferred_element_type=jnp.float32)


def product_of_rows(left, right):
    return lax.dot_general(left, right, (((1,), (1,)), ((), ())), precision=HIGHEST,
                           preferred_element_type=jnp.float32)


def orthonormal_kernel(rows_ref, out_ref):
    rows = rows_ref[...]
    out_ref[...] = product(inverse_factor(product_of_rows(rows, rows)), rows)


def iteration_kernel(gram_ref, rows_ref, field_ref, core_ref, current):
    current[...] = product(rows_ref[...], gram_ref[...])

    def sweep(index, carry):
        rows = current[...]
        factor = inverse_factor(product_of_rows(rows, rows))
        current[...] = product(factor, product(rows, gram_ref[...]))
        return carry

    lax.fori_loop(0, ITERS - 1, sweep, 0)
    rows = current[...]
    subspace = product(inverse_factor(product_of_rows(rows, rows)), rows)
    core_ref[...] = product_of_rows(field_ref[...], subspace)


VMEM = pl.BlockSpec(memory_space=pltpu.VMEM)


def transposed_product(left, right):
    return lax.dot_general(left, right, (((0,), (0,)), ((), ())), precision=HIGHEST)


def shards(field, start_block):
    cells_two, cells_three, order_one = field.shape
    unfolded = field.reshape(cells_two * cells_three, order_one)
    start_rows = pl.pallas_call(
        orthonormal_kernel,
        out_shape=jax.ShapeDtypeStruct((RANK, order_one), jnp.float32),
        in_specs=[VMEM],
        out_specs=VMEM,
    )(start_block.T)
    gram_local = transposed_product(unfolded, unfolded)
    gram_whole = lax.psum(gram_local, ("narrow", "wide"))
    core_cells = pl.pallas_call(
        iteration_kernel,
        out_shape=jax.ShapeDtypeStruct((cells_two * cells_three, RANK), jnp.float32),
        in_specs=[VMEM, VMEM, VMEM],
        out_specs=VMEM,
        scratch_shapes=[pltpu.VMEM((RANK, order_one), jnp.float32)],
        compiler_params=pltpu.CompilerParams(vmem_limit_bytes=48 << 20),
    )(gram_whole, start_rows, unfolded)
    core_block = core_cells.reshape(cells_two, cells_three, RANK)
    regrouped = lax.all_to_all(core_block, "narrow", split_axis=2, concat_axis=0, tiled=True)
    merged = regrouped.reshape(regrouped.shape[0], regrouped.shape[1] * regrouped.shape[2])
    gram_part = jnp.dot(merged, merged.T, precision=HIGHEST)
    sectioned = lax.psum_scatter(gram_part, "narrow", scatter_dimension=0, tiled=True)
    finished = lax.psum_scatter(sectioned, "wide", scatter_dimension=1, tiled=True)
    return finished / (RANK * B3 * lax.axis_size("wide"))


def solution(mesh):
    return jax.shard_map(
        shards,
        mesh=mesh,
        in_specs=(P("narrow", "wide", None), P()),
        out_specs=P("narrow", "wide"),
        check_vma=False,
    )
```

time: 631 us -> 537 us (0.85)
  the two profiles are of different devices: /device:TPU:64 before, /device:TPU:6 now
where the time goes in v1:
time: 537 us; the launch traced here: 526 us
  waiting for transfers between devices  377 us (70%)
  blocking collectives  76.2 us (14%)
  Pallas kernels  38.8 us (7%)
  between operations  14.7 us (3%)
  local copies, waits for them, and re-layouts  11.2 us (2%)
  matrix products  7.53 us (1%)
    psum x1, waiting for transfers between devices, shards(): gram_whole = lax.psum(gram_local, ('narrow', 'wide'))  280 us
    unnamed x3, waiting for transfers between devices  96.9 us
    unnamed x1, blocking collectives  63 us
    pallas_call x1, Pallas kernels, shards(): pl.pallas_call(iteration_kernel, out_shape=jax.ShapeDtypeStruct((cells_tw...  30.3 us
    all_to_all x1, blocking collectives, shards(): lax.all_to_all(core_block, 'narrow', split_axis=2, concat_axis=0, tiled=T...  13.2 us
  transfers between devices with their start and end apart: 2, of which 2 were waited for; matrix products, arithmetic and copies ran while one was open for 1% of the time, Pallas kernels for 2%

profile of v1, /device:TPU:6, one launch (start us, length us, event | category | flops | bytes accessed | tf_op | source)
XLA Modules:
  0.0 526.4 jit_solution(4721428270000292910)
XLA Ops:
  6.5 0.0 all-reduce.5.cloned.1.call-start
  6.5 6.6 %convolution_bitcast_fusion = f32[1024,1024]{1,0:T(8,128)} fusion(f32[8,16,1024]{2,1,0:T(8,128)} %param.2), kind=kOutput, calls=%fused_computation | convolution fusion | flops 1610612736 | bytes 4718592 | tf_op jit(solution)/shard_map/dot_general | solution.py:101
  13.2 0.0 copy-start.3
  13.2 0.0 copy-start.2
  13.2 0.0 all-reduce.5.cloned.1.call-update
  13.2 0.0 all-reduce.7.cloned.1.call-start
  13.3 1.0 copy-done.3
  14.2 1.1 copy.9
  15.3 8.5 %shard_map.28.rows_ref = f32[128,1024]{1,0:T(8,128)} custom-call(f32[128,1024]{1,0:T(8,128)} %bitcast.24), custom_call_target="tpu_custom_call" | custom-call | tf_op jit(solution)/shard_map/pallas_call | solution.py:107
  23.8 280.2 %all-reduce.5.cloned.1.call-done.gram_ref = f32[1024,1024]{1,0:T(8,128)} async-done(((f32[1024,1024]{1,0:T(8,128)}), f32[1024,1024]{1,0:T(8,128)}) %all-reduce.5.cloned.1.call-update) | async-done | bytes 4194320 | tf_op jit(solution)/shard_map/psum | solution.py:114
  304.0 0.0 copy-done.2
  304.0 0.0 copy-start
  304.0 2.2 copy-done
  306.2 1.0 copy-done.1
  307.3 30.3 %shard_map.29 = f32[128,128]{1,0:T(8,128)S(1)} custom-call(f32[1024,1024]{1,0:T(8,128)S(1)} %copy-done, f32[128,1024]{1,0:T(8,128)S(1)} %copy-done.1, f32[128,1024]{1,0:T(8,128)S(1)} %bitcast.20), custom_call_target="tpu_custom_call" | custom-call | tf_op jit(solution)/shard_map/pallas_call | solution.py:115
  337.5 0.2 copy.10
  337.8 0.2 reshape.18
  338.0 13.2 %all_to_all.15 = f32[16,1,1024]{2,1,0:T(1,128)S(1)} all-to-all(f32[16,1,1024]{2,1,0:T(1,128)S(1)} %reshape.18), channel_id=1, replica_groups=mesh['narrow'=16,'wide'=32] {'narrow'}, dimensions={0} | all-to-all | bytes 131072 | tf_op jit(solution)/shard_map/all_to_all | solution.py:124
  351.2 0.5 broadcast.1
  351.7 0.8 reduce
  352.5 0.2 reshape.19
  352.7 0.4 copy.12
  353.1 0.5 reshape.12
  353.6 0.9 fusion
  354.5 0.0 all-reduce.7.cloned.1.call-update
  354.5 1.3 dynamic-slice
  355.8 1.3 dynamic-slice.2
  358.3 96.9 %all-reduce.7.cloned.1.call-done = f32[128,128]{1,0:T(8,128)} async-done(((f32[128,128]{1,0:T(8,128)}), f32[128,128]{1,0:T(8,128)}) %all-reduce.7.cloned.1.call-update) | async-done | bytes 65552
  455.1 0.7 constant_dynamic-slice_fusion
  455.8 63.0 %all-reduce.1 = f32[8,128]{1,0:T(8,128)S(1)} all-reduce(f32[8,128]{1,0:T(8,128)S(1)} %constant_dynamic-slice_fusion), channel_id=3, replica_groups=mesh['narrow'=16,'wide'=32] {'wide'}, use_global_device_ids=true, to_apply=%region_2.0.clone | all-reduce | flops 1024 | bytes 8192
  518.8 0.1 dynamic-slice_multiply_fusion
  518.9 0.7 copy.13
  (1 shorter events, 0.0 us)
Async XLA Ops:
  6.5 297.5 %all-reduce.5.cloned.1.call-start = ((), (), s32[]{:S(2)}) async-start(), calls=%async_computation.1 | async-start | bytes 8388608 | tf_op jit(solution)/shard_map/psum | solution.py:114
  13.2 1.0 copy-start.3
  13.2 290.8 %copy-start.2 = (f32[8,16,1024]{2,1,0:T(8,128)S(1)}, f32[8,16,1024]{2,1,0:T(8,128)}, u32[]{:S(2)}) copy-start(f32[8,16,1024]{2,1,0:T(8,128)} %param.2) | copy-start | bytes 1572868
  13.2 441.9 %all-reduce.7.cloned.1.call-start = ((), (), s32[]{:S(2)}) async-start(), calls=%async_computation.2 | async-start | bytes 131072
  304.0 2.2 copy-start
  306.2 1.0 copy-start.1
Sparse Core Ops, SparseCore 0:
  13.3 290.6 all-reduce.4
  354.6 100.4 all-reduce.6

commit v2 on v1

--- a/solution.py
+++ b/solution.py
@@ -1,3 +1,5 @@
+import functools
+
 import jax
 import jax.numpy as jnp
 from jax import lax
@@ -11,6 +13,17 @@
 ROWS = 8
 LANES = 128
 HIGHEST = lax.Precision.HIGHEST
+MESH_ID = pl.DeviceIdType.MESH
+
+CORES = 2
+CHIPS_Y = 8
+
+TILE = 256
+TILE_ROWS = TILE * TILE // LANES
+TILES = (((0, 0), (0, 1), (0, 2), (0, 3), (1, 1)), ((1, 2), (1, 3), (2, 2), (2, 3), (3, 3)))
+HALF_ROWS = TILE_ROWS * len(TILES[0])
+
+GROUPS = (("zyx", (0, 1)), ("yzx", (2, 3)), ("xyz", (4,)))
 
 
 def lane_copy(block, lane):
@@ -74,18 +87,306 @@
                            preferred_element_type=jnp.float32)
 
 
+def product_of_columns(left, right):
+    return lax.dot_general(left.T, right, (((1,), (0,)), ((), ())), precision=HIGHEST,
+                           preferred_element_type=jnp.float32)
+
+
+class Place:
+    def __init__(self, chips):
+        self.chips = chips
+        self.narrow, self.wide = lax.axis_index("narrow"), lax.axis_index("wide")
+        self.core = self.narrow % CORES
+        self.at = {"z": self.narrow // CORES, "y": self.wide % chips["y"], "x": self.wide // chips["y"]}
+
+    def step(self, axis, offset):
+        return (self.at[axis] + offset + self.chips[axis]) % self.chips[axis]
+
+    def device(self, axis, position):
+        if axis == "z":
+            return (position * CORES + self.core, self.wide)
+        if axis == "y":
+            return (self.narrow, self.at["x"] * self.chips["y"] + position)
+        return (self.narrow, position * self.chips["y"] + self.at["y"])
+
+    def partner(self):
+        return (self.narrow + 1 - 2 * self.core, self.wide)
+
+    def along(self, axis):
+        return [self.device(axis, self.step(axis, offset)) for offset in range(1, self.chips[axis])]
+
+
+class Copies:
+    def __init__(self, send_sem, recv_sem):
+        self.send_sem, self.recv_sem, self.started = send_sem, recv_sem, []
+
+    def start(self, source, target, device):
+        index = len(self.started)
+        copy = pltpu.make_async_remote_copy(source, target, self.send_sem.at[index], self.recv_sem.at[index],
+                                            device_id=device, device_id_type=MESH_ID)
+        copy.start()
+        self.started.append(copy)
+        return copy
+
+    def drain(self):
+        for copy in self.started:
+            copy.wait_send()
+
+
+def greet(devices):
+    barrier = pltpu.get_barrier_semaphore()
+    for device in devices:
+        pl.semaphore_signal(barrier, inc=1, device_id=device, device_id_type=MESH_ID)
+    pl.semaphore_wait(barrier, len(devices))
+
+
+def aligned(start, size):
+    return pl.ds(pl.multiple_of(start, ROWS), size)
+
+
+class Group:
+    def __init__(self, chips, axes, tiles):
+        self.first, self.second, self.third = axes
+        self.tiles = tiles
+        self.ring = chips[self.first]
+        self.ahead, self.behind = self.ring // 2, (self.ring - 1) // 2
+        self.block = TILE_ROWS // self.ring
+        self.piece = self.block // chips[self.second]
+        self.rows = self.piece * len(tiles)
+        self.chips = chips
+
+    def scratch(self):
+        def rows(*shape):
+            return pltpu.VMEM((*shape, LANES), jnp.float32)
+
+        count, second = len(self.tiles), self.chips[self.second]
+        return [rows(count, self.ahead, self.block), rows(count, max(self.behind, 1), self.block),
+                rows(second, self.rows), rows(max(second - 1, 1), self.rows),
+                rows(self.chips[self.third], self.rows), rows(second, self.rows)]
+
+    def copies(self):
+        links = len(self.tiles) * (self.ring - 1)
+        return 2 * links + 2 * (self.chips[self.second] - 1) + self.chips[self.third] - 1
+
+    def take(self, refs):
+        self.up, self.down, self.sums, self.parts, self.slots, self.gathered = refs
+
+    def rows_of(self, tile, position):
+        return aligned(tile * TILE_ROWS + position * self.block, self.block)
+
+
+def gram_kernel(chips, field_ref, out_ref, joined, mine, *rest):
+    groups = [Group(chips, axes, tiles) for axes, tiles in GROUPS]
+    for number, group in enumerate(groups):
+        group.take(rest[6 * number:6 * number + 6])
+    copies = Copies(*rest[6 * len(groups):])
+    place = Place(chips)
+    core = place.core
+    greet([place.partner()] + [device for axis in "zyx" for device in place.along(axis)])
+
+    depth = field_ref.shape[0]
+    own = aligned(core * depth, depth)
+    exchange = copies.start(field_ref, joined.at[own, :], place.partner())
+    joined[own, :] = field_ref[...]
+    exchange.wait_recv()
+
+    moving = {}
+
+    def send_ahead(group, tile, source, step):
+        device = place.device(group.first, place.step(group.first, 1))
+        moving[tile, "up", step] = copies.start(source, group.up.at[group.tiles.index(tile), step], device)
+
+    def send_behind(group, tile, source, step):
+        device = place.device(group.first, place.step(group.first, -1))
+        moving[tile, "down", step] = copies.start(source, group.down.at[group.tiles.index(tile), step], device)
+
+    order = [(group, group.tiles[turn]) for turn in range(2) for group in groups if turn < len(group.tiles)]
+    for group, tile in order:
+        rows, columns = (TILES[0][tile][side] + core * (TILES[1][tile][side] - TILES[0][tile][side])
+                         for side in range(2))
+        block = product_of_columns(joined[:, pl.ds(pl.multiple_of(rows * TILE, TILE), TILE)],
+                                   joined[:, pl.ds(pl.multiple_of(columns * TILE, TILE), TILE)])
+        for half in range(TILE // LANES):
+            start = tile * TILE_ROWS + half * TILE
+            mine[start:start + TILE, :] = block[:, half * LANES:(half + 1) * LANES]
+        send_ahead(group, tile, mine.at[group.rows_of(tile, place.step(group.first, group.ahead)), :], 0)
+        if group.behind:
+            send_behind(group, tile, mine.at[group.rows_of(tile, place.step(group.first, -group.behind)), :], 0)
+
+    pieces = {}
+    for step in range(1, max(group.ahead for group in groups) + 1):
+        for group, tile in order:
+            index = group.tiles.index(tile)
+            if step < group.ahead:
+                moving[tile, "up", step - 1].wait_recv()
+                target = place.step(group.first, group.ahead - step)
+                group.up[index, step - 1] = group.up[index, step - 1] + mine[group.rows_of(tile, target), :]
+                send_ahead(group, tile, group.up.at[index, step - 1], step)
+            if step < group.behind:
+                moving[tile, "down", step - 1].wait_recv()
+                target = place.step(group.first, step - group.behind)
+                group.down[index, step - 1] = group.down[index, step - 1] + mine[group.rows_of(tile, target), :]
+                send_behind(group, tile, group.down.at[index, step - 1], step)
+            if step == group.ahead:
+                moving[tile, "up", step - 1].wait_recv()
+                total = mine[group.rows_of(tile, place.at[group.first]), :] + group.up[index, step - 1]
+                if group.behind:
+                    moving[tile, "down", group.behind - 1].wait_recv()
+                    total = total + group.down[index, group.behind - 1]
+                for part in range(chips[group.second]):
+                    group.sums[part, index * group.piece:(index + 1) * group.piece, :] = (
+                        total[part * group.piece:(part + 1) * group.piece, :])
+                if index == len(group.tiles) - 1:
+                    pieces[group] = []
+                    for offset in range(1, chips[group.second]):
+                        to = place.step(group.second, offset)
+                        pieces[group].append(copies.start(group.sums.at[to], group.parts.at[offset - 1],
+                                                          place.device(group.second, to)))
+
+    arrival = sorted(groups, key=lambda group: group.ahead)
+    for group in arrival:
+        total = group.sums[place.at[group.second]]
+        for number, copy in enumerate(pieces[group]):
+            copy.wait_recv()
+            total = total + group.parts[number]
+        here = place.at[group.third]
+        group.slots[here] = total
+        pieces[group] = [copies.start(group.slots.at[here], group.slots.at[here], device)
+                         for device in place.along(group.third)]
+    for group in arrival:
+        for copy in pieces[group]:
+            copy.wait_recv()
+        total = group.slots[0]
+        for slot in range(1, chips[group.third]):
+            total = total + group.slots[slot]
+        here = place.at[group.second]
+        group.gathered[here] = total
+        pieces[group] = [copies.start(group.gathered.at[here], group.gathered.at[here], device)
+                         for device in place.along(group.second)]
+
+    def pass_on(group, tile, way, step):
+        sign = 1 if way == "up" else -1
+        rows = group.rows_of(tile, place.step(group.first, -sign * step))
+        device = place.device(group.first, place.step(group.first, sign))
+        moving[tile, way, step] = copies.start(out_ref.at[core, rows, :], out_ref.at[core, rows, :], device)
+
+    for group in arrival:
+        for copy in pieces[group]:
+            copy.wait_recv()
+        for index, tile in enumerate(group.tiles):
+            start = tile * TILE_ROWS + place.at[group.first] * group.block
+            for part in range(chips[group.second]):
+                out_ref[core, aligned(start + part * group.piece, group.piece), :] = (
+                    group.gathered[part, index * group.piece:(index + 1) * group.piece, :])
+            pass_on(group, tile, "up", 0)
+            if group.behind:
+                pass_on(group, tile, "down", 0)
+    crossing = []
+    for step in range(1, max(group.ahead for group in groups) + 1):
+        for group, tile in order:
+            if step <= group.ahead:
+                moving[tile, "up", step - 1].wait_recv()
+                if step < group.ahead:
+                    pass_on(group, tile, "up", step)
+            if step <= group.behind:
+                moving[tile, "down", step - 1].wait_recv()
+                if step < group.behind:
+                    pass_on(group, tile, "down", step)
+            if step == group.ahead:
+                rows = pl.ds(tile * TILE_ROWS, TILE_ROWS)
+                crossing.append(copies.start(out_ref.at[core, rows, :], out_ref.at[core, rows, :], place.partner()))
+    for copy in crossing:
+        copy.wait_recv()
+    copies.drain()
+
+
+def gram_everywhere(field_rows, chips):
+    groups = [Group(chips, axes, tiles) for axes, tiles in GROUPS]
+    depth, order = field_rows.shape
+    count = 1 + len(TILES[0]) + sum(group.copies() for group in groups)
+    return pl.pallas_call(
+        functools.partial(gram_kernel, chips),
+        out_shape=jax.ShapeDtypeStruct((CORES, HALF_ROWS, LANES), jnp.float32),
+        in_specs=[VMEM],
+        out_specs=VMEM,
+        scratch_shapes=[pltpu.VMEM((CORES * depth, order), jnp.float32), pltpu.VMEM((HALF_ROWS, LANES), jnp.float32)]
+        + [shape for group in groups for shape in group.scratch()]
+        + [pltpu.SemaphoreType.DMA((count,)), pltpu.SemaphoreType.DMA((count,))],
+        compiler_params=pltpu.CompilerParams(collective_id=0, has_side_effects=True, vmem_limit_bytes=48 << 20),
+    )(field_rows)
+
+
+def mode_two_kernel(chips, core_ref, out_ref, leaving, cells, split, terms, rows_y, rows_x, send_sem, recv_sem):
+    place, copies = Place(chips), Copies(send_sem, recv_sem)
+    devices = CORES * chips["z"]
+    others = [(place.narrow + offset) % devices for offset in range(1, devices)]
+    greet([(narrow, place.wide) for narrow in others] + place.along("y") + place.along("x"))
+
+    def regroup(source, target):
+        target[place.narrow] = source[place.narrow]
+        return [copies.start(source.at[narrow], target.at[place.narrow], (narrow, place.wide)) for narrow in others]
+
+    def sum_along(axis, slots, term):
+        slots[place.at[axis]] = term
+        here = slots.at[place.at[axis]]
+        for copy in [copies.start(here, here, device) for device in place.along(axis)]:
+            copy.wait_recv()
+        return functools.reduce(lambda total, slot: total + slots[slot], range(1, chips[axis]), slots[0])
+
+    for index in range(devices):
+        leaving[index] = core_ref[pl.ds(index, ROWS, stride=devices), :]
+    for copy in regroup(leaving, cells):
+        copy.wait_recv()
+    block = cells[...].reshape(devices * ROWS, RANK)
+    split[...] = product_of_rows(block, block).reshape(devices, ROWS, devices * ROWS)
+    for copy in regroup(split, terms):
+        copy.wait_recv()
+    total = functools.reduce(lambda total, slot: total + terms[slot], range(1, devices), terms[0])
+    total = sum_along("y", rows_y, total)
+    out_ref[...] = sum_along("x", rows_x, total)
+    copies.drain()
+
+
+def mode_two_rows(core_cells, chips):
+    devices = CORES * chips["z"]
+    width = devices * ROWS
+    count = 2 * (devices - 1) + chips["y"] + chips["x"] - 2
+
+    def tiles(number, lanes):
+        return pltpu.VMEM((number, ROWS, lanes), jnp.float32)
+
+    return pl.pallas_call(
+        functools.partial(mode_two_kernel, chips),
+        out_shape=jax.ShapeDtypeStruct((ROWS, width), jnp.float32),
+        in_specs=[VMEM],
+        out_specs=VMEM,
+        scratch_shapes=[tiles(devices, RANK), tiles(devices, RANK), tiles(devices, width), tiles(devices, width),
+                        tiles(chips["y"], width), tiles(chips["x"], width),
+                        pltpu.SemaphoreType.DMA((count,)), pltpu.SemaphoreType.DMA((count,))],
+        compiler_params=pltpu.CompilerParams(collective_id=1, has_side_effects=True),
+    )(core_cells)
+
+
 def orthonormal_kernel(rows_ref, out_ref):
     rows = rows_ref[...]
     out_ref[...] = product(inverse_factor(product_of_rows(rows, rows)), rows)
 
 
-def iteration_kernel(gram_ref, rows_ref, field_ref, core_ref, current):
-    current[...] = product(rows_ref[...], gram_ref[...])
+def iteration_kernel(tiles_ref, rows_ref, field_ref, core_ref, gram, current):
+    for side in range(CORES):
+        for number, (row, column) in enumerate(TILES[side]):
+            start = number * TILE_ROWS
+            tile = jnp.concatenate([tiles_ref[side, start:start + TILE, :],
+                                    tiles_ref[side, start + TILE:start + 2 * TILE, :]], axis=1)
+            gram[row * TILE:(row + 1) * TILE, column * TILE:(column + 1) * TILE] = tile
+            if row != column:
+                gram[column * TILE:(column + 1) * TILE, row * TILE:(row + 1) * TILE] = tile.T
+    current[...] = product(rows_ref[...], gram[...])
 
     def sweep(index, carry):
         rows = current[...]
         factor = inverse_factor(product_of_rows(rows, rows))
-        current[...] = product(factor, product(rows, gram_ref[...]))
+        current[...] = product(factor, product(rows, gram[...]))
         return carry
 
     lax.fori_loop(0, ITERS - 1, sweep, 0)
@@ -97,11 +398,7 @@
 VMEM = pl.BlockSpec(memory_space=pltpu.VMEM)
 
 
-def transposed_product(left, right):
-    return lax.dot_general(left, right, (((0,), (0,)), ((), ())), precision=HIGHEST)
-
-
-def shards(field, start_block):
+def shards(chips, field, start_block):
     cells_two, cells_three, order_one = field.shape
     unfolded = field.reshape(cells_two * cells_three, order_one)
     start_rows = pl.pallas_call(
@@ -110,28 +407,25 @@
         in_specs=[VMEM],
         out_specs=VMEM,
     )(start_block.T)
-    gram_local = transposed_product(unfolded, unfolded)
-    gram_whole = lax.psum(gram_local, ("narrow", "wide"))
+    gram_tiles = gram_everywhere(unfolded, chips)
     core_cells = pl.pallas_call(
         iteration_kernel,
         out_shape=jax.ShapeDtypeStruct((cells_two * cells_three, RANK), jnp.float32),
         in_specs=[VMEM, VMEM, VMEM],
         out_specs=VMEM,
-        scratch_shapes=[pltpu.VMEM((RANK, order_one), jnp.float32)],
+        scratch_shapes=[pltpu.VMEM((order_one, order_one), jnp.float32), pltpu.VMEM((RANK, order_one), jnp.float32)],
         compiler_params=pltpu.CompilerParams(vmem_limit_bytes=48 << 20),
-    )(gram_whole, start_rows, unfolded)
-    core_block = core_cells.reshape(cells_two, cells_three, RANK)
-    regrouped = lax.all_to_all(core_block, "narrow", split_axis=2, concat_axis=0, tiled=True)
-    merged = regrouped.reshape(regrouped.shape[0], regrouped.shape[1] * regrouped.shape[2])
-    gram_part = jnp.dot(merged, merged.T, precision=HIGHEST)
-    sectioned = lax.psum_scatter(gram_part, "narrow", scatter_dimension=0, tiled=True)
-    finished = lax.psum_scatter(sectioned, "wide", scatter_dimension=1, tiled=True)
+    )(gram_tiles, start_rows, unfolded)
+    rows = mode_two_rows(core_cells, chips)
+    columns = rows.shape[1] // lax.axis_size("wide")
+    finished = lax.dynamic_slice_in_dim(rows, lax.axis_index("wide") * columns, columns, axis=1)
     return finished / (RANK * B3 * lax.axis_size("wide"))
 
 
-def solution(mesh):
+def solution(mesh, chips_y=CHIPS_Y):
+    chips = {"z": mesh.shape["narrow"] // CORES, "y": chips_y, "x": mesh.shape["wide"] // chips_y}
     return jax.shard_map(
-        shards,
+        functools.partial(shards, chips),
         mesh=mesh,
         in_specs=(P("narrow", "wide", None), P()),
         out_specs=P("narrow", "wide"),

time: 537 us -> 132 us (0.25); the launches traced: 526 us -> 131 us
  waiting for transfers between devices: 377 us -> 0 us
  Pallas kernels: 38.8 us -> 126 us
  blocking collectives: 76.2 us -> 0 us
  between operations: 14.7 us -> 0.04 us
  matrix products: 7.53 us -> 0 us
  local copies, waits for them, and re-layouts: 11.2 us -> 4.35 us
    psum x1 -> x0, waiting for transfers between devices: 280 us -> none  [shards(): gram_whole = lax.psum(gram_local, ('narrow', 'wide'))]
    unnamed x3 -> x0, waiting for transfers between devices: 96.9 us -> none
    pallas_call x0 -> x2, Pallas kernels: none -> 87 us  [the longest x1 62.5 us: gram_everywhere(): pl.pallas_call(functools.partial(gram_kernel, chips), out_shape=jax.Shape...]
    unnamed x1 -> x0, blocking collectives: 63 us -> none
    all_to_all x1 -> x0, blocking collectives: 13.2 us -> none  [shards(): lax.all_to_all(core_block, 'narrow', split_axis=2, concat_axis=0, tiled=T...]
    dot_general x2 -> x0, matrix products: 7.53 us -> none  [the longest x1 6.64 us: transposed_product(): lax.dot_general(left, right, (((0,), (0,)), ((), ())), precision=HIGHEST)]
  transfers between devices with their start and end apart: 2 -> 0, of which waited for: 2 -> 0; matrix products, arithmetic and copies ran while one was open for 1% -> 0% of each run, Pallas kernels for 2% -> 0%
where the time goes in v2:
time: 132 us; the launch traced here: 131 us
  Pallas kernels  126 us (95%)
  local copies, waits for them, and re-layouts  4.35 us (3%)
    pallas_call x1, Pallas kernels, gram_everywhere(): pl.pallas_call(functools.partial(gram_kernel, chips), out_shape=jax.Shape...  62.5 us
    pallas_call x1, Pallas kernels, shards(): pl.pallas_call(iteration_kernel, out_shape=jax.ShapeDtypeStruct((cells_tw...  30.5 us
    pallas_call x1, Pallas kernels, mode_two_rows(): pl.pallas_call(functools.partial(mode_two_kernel, chips), out_shape=jax.S...  24.5 us
    pallas_call x1, Pallas kernels, shards(): pl.pallas_call(orthonormal_kernel, out_shape=jax.ShapeDtypeStruct((RANK,...  8.49 us
    unnamed x7, local copies, waits for them, and re-layouts  3.7 us

profile of v2, /device:TPU:6, one launch (start us, length us, event | category | flops | bytes accessed | tf_op | source)
XLA Modules:
  0.0 131.1 jit_solution(9058395155172110719)
XLA Ops:
  0.0 2.0 %copy.3 = f32[1024,128]{0,1:T(8,128)} copy(f32[1024,128]{1,0:T(8,128)} %param.3) | data formatting | bytes 1048576 | tf_op args[1]
  2.0 8.5 %shard_map.29.rows_ref = f32[128,1024]{1,0:T(8,128)} custom-call(f32[128,1024]{1,0:T(8,128)} %bitcast.4), custom_call_target="tpu_custom_call" | custom-call | tf_op jit(solution)/shard_map/pallas_call | solution.py:404
  10.5 0.0 copy-start.1
  10.5 1.0 copy-done.1
  11.6 0.0 copy-start
  11.6 62.5 %shard_map.28.tiles_ref = f32[2,2560,128]{2,1,0:T(8,128)S(1)} custom-call(f32[128,1024]{1,0:T(8,128)S(1)} %bitcast.2), custom_call_target="tpu_custom_call" | custom-call | tf_op jit(solution)/shard_map/pallas_call | solution.py:307
  74.1 0.0 copy-done
  74.1 30.5 %shard_map.30.core_ref = f32[128,128]{1,0:T(8,128)S(1)} custom-call(f32[2,2560,128]{2,1,0:T(8,128)S(1)} %shard_map.28.tiles_ref, f32[128,1024]{1,0:T(8,128)S(1)} %copy-done, f32[128,1024]{1,0:T(8,128)S(1)} %bitcast.3), custom_call_target="tpu_custom_call" | custom-call | tf_op jit(solution)/shard_map/pallas_call | solution.py:411
  104.6 0.0 copy-start.2
  104.6 0.6 copy-done.2
  105.2 24.5 %shard_map.31 = f32[8,128]{1,0:T(8,128)} custom-call(f32[128,128]{1,0:T(8,128)} %copy-done.2), custom_call_target="tpu_custom_call" | custom-call | tf_op jit(solution)/shard_map/pallas_call | solution.py:358
  129.7 0.8 dynamic-slice_multiply_fusion
  130.4 0.7 copy.4
Async XLA Ops:
  10.5 1.0 copy-start.1
  11.6 62.5 %copy-start = (f32[128,1024]{1,0:T(8,128)S(1)}, f32[128,1024]{1,0:T(8,128)}, u32[]{:S(2)}) copy-start(f32[128,1024]{1,0:T(8,128)} %shard_map.29.rows_ref) | copy-start | bytes 1572868
  104.6 0.6 copy-start.2

commit v3 on v2

--- a/solution.py
+++ b/solution.py
@@ -8,7 +8,6 @@
 from jax.sharding import PartitionSpec as P
 
 RANK = 128
-B3 = 16
 ITERS = 4
 ROWS = 8
 LANES = 128
@@ -41,7 +40,7 @@
     return terms[0]
 
 
-def inverse_factor(gram):
+def factor_panels(gram):
     row = lax.broadcasted_iota(jnp.int32, (ROWS, LANES), 0)
     lane = lax.broadcasted_iota(jnp.int32, (ROWS, LANES), 1)
     panels = RANK // ROWS
@@ -49,7 +48,7 @@
     right = [jnp.where(lane == row + ROWS * p, 1.0, 0.0) for p in range(panels)]
     finished = []
     for p in range(panels):
-        diag = [lane_copy(left[p], ROWS * p + c) for c in range(ROWS)]
+        diag = [jnp.where(row < ROWS, lane_copy(left[p], ROWS * p + c), 0.0) for c in range(ROWS)]
         scaled = [jnp.zeros((ROWS, LANES), jnp.float32) for _ in range(ROWS)]
         for j in range(ROWS):
             pivot = row_copy(diag[j], j)
@@ -70,11 +69,22 @@
         finished.append(tree_sum(scaled[c] * row_copy(right[p], c) for c in range(ROWS)))
         left_rows = [row_copy(solved_left, c) for c in range(ROWS)]
         right_rows = [row_copy(solved_right, c) for c in range(ROWS)]
-        for q in range(p + 1, panels):
-            factors = [lane_copy(left[q], ROWS * p + c) for c in range(ROWS)]
-            left[q] = left[q] - tree_sum(factors[c] * left_rows[c] for c in range(ROWS))
-            right[q] = right[q] - tree_sum(factors[c] * right_rows[c] for c in range(ROWS))
+        later = range(p + 1, panels)
+        factors = [[lane_copy(left[q], ROWS * p + c) for q in later] for c in range(ROWS)]
+        for number, q in enumerate(later):
+            left[q] = left[q] - tree_sum(factors[c][number] * left_rows[c] for c in range(ROWS))
+            right[q] = right[q] - tree_sum(factors[c][number] * right_rows[c] for c in range(ROWS))
+        yield
     return jnp.concatenate(finished, axis=0)
+
+
+def inverse_factor(gram):
+    panels = factor_panels(gram)
+    while True:
+        try:
+            next(panels)
+        except StopIteration as stop:
+            return stop.value
 
 
 def product(left, right):
@@ -131,13 +141,6 @@
     def drain(self):
         for copy in self.started:
             copy.wait_send()
-
-
-def greet(devices):
-    barrier = pltpu.get_barrier_semaphore()
-    for device in devices:
-        pl.semaphore_signal(barrier, inc=1, device_id=device, device_id_type=MESH_ID)
-    pl.semaphore_wait(barrier, len(devices))
 
 
 def aligned(start, size):
@@ -175,19 +178,41 @@
         return aligned(tile * TILE_ROWS + position * self.block, self.block)
 
 
-def gram_kernel(chips, field_ref, out_ref, joined, mine, *rest):
+def start_rows(rows_ref):
+    factor = yield from factor_panels(product_of_rows(rows_ref[...], rows_ref[...]))
+    rows_ref[...] = product(factor, rows_ref[...])
+
+
+def hosvd_kernel(chips, field_ref, start_ref, out_ref, joined, mine, tiles_ref, gram, current, leaving, cells, split,
+                 terms, rows_y, rows_x, *rest):
     groups = [Group(chips, axes, tiles) for axes, tiles in GROUPS]
     for number, group in enumerate(groups):
         group.take(rest[6 * number:6 * number + 6])
     copies = Copies(*rest[6 * len(groups):])
     place = Place(chips)
     core = place.core
-    greet([place.partner()] + [device for axis in "zyx" for device in place.along(axis)])
+    devices = CORES * chips["z"]
+    others = [(place.narrow + offset) % devices for offset in range(1, devices)]
+
+    barrier = pltpu.get_barrier_semaphore()
+    greeted = [(narrow, place.wide) for narrow in others] + place.along("y") + place.along("x")
+    for device in greeted:
+        pl.semaphore_signal(barrier, inc=1, device_id=device, device_id_type=MESH_ID)
+    current[...] = start_ref[...].T
+    leaving[...] = jnp.swapaxes(field_ref[...].reshape(ROWS, devices, field_ref.shape[1]), 0, 1)
+    pl.semaphore_wait(barrier, len(greeted))
 
     depth = field_ref.shape[0]
     own = aligned(core * depth, depth)
     exchange = copies.start(field_ref, joined.at[own, :], place.partner())
     joined[own, :] = field_ref[...]
+    starting = start_rows(current)
+
+    def advance(panels):
+        for _ in range(panels):
+            next(starting, None)
+
+    advance(1)
     exchange.wait_recv()
 
     moving = {}
@@ -215,6 +240,7 @@
 
     pieces = {}
     for step in range(1, max(group.ahead for group in groups) + 1):
+        advance(2)
         for group, tile in order:
             index = group.tiles.index(tile)
             if step < group.ahead:
@@ -244,6 +270,7 @@
                                                           place.device(group.second, to)))
 
     arrival = sorted(groups, key=lambda group: group.ahead)
+    advance(3)
     for group in arrival:
         total = group.sums[place.at[group.second]]
         for number, copy in enumerate(pieces[group]):
@@ -253,6 +280,7 @@
         group.slots[here] = total
         pieces[group] = [copies.start(group.slots.at[here], group.slots.at[here], device)
                          for device in place.along(group.third)]
+    advance(3)
     for group in arrival:
         for copy in pieces[group]:
             copy.wait_recv()
@@ -268,20 +296,30 @@
         sign = 1 if way == "up" else -1
         rows = group.rows_of(tile, place.step(group.first, -sign * step))
         device = place.device(group.first, place.step(group.first, sign))
-        moving[tile, way, step] = copies.start(out_ref.at[core, rows, :], out_ref.at[core, rows, :], device)
-
+        moving[tile, way, step] = copies.start(tiles_ref.at[core, rows, :], tiles_ref.at[core, rows, :], device)
+
+    advance(RANK)
     for group in arrival:
         for copy in pieces[group]:
             copy.wait_recv()
         for index, tile in enumerate(group.tiles):
             start = tile * TILE_ROWS + place.at[group.first] * group.block
             for part in range(chips[group.second]):
-                out_ref[core, aligned(start + part * group.piece, group.piece), :] = (
+                tiles_ref[core, aligned(start + part * group.piece, group.piece), :] = (
                     group.gathered[part, index * group.piece:(index + 1) * group.piece, :])
             pass_on(group, tile, "up", 0)
             if group.behind:
                 pass_on(group, tile, "down", 0)
-    crossing = []
+    def unpack(side, tile):
+        row, column = (pl.multiple_of((TILES[0][tile][way] + side * (TILES[1][tile][way] - TILES[0][tile][way])) * TILE,
+                                      TILE) for way in range(2))
+        start = tile * TILE_ROWS
+        block = jnp.concatenate([tiles_ref[side, start:start + TILE, :],
+                                 tiles_ref[side, start + TILE:start + 2 * TILE, :]], axis=1)
+        gram[pl.ds(row, TILE), pl.ds(column, TILE)] = block
+        gram[pl.ds(column, TILE), pl.ds(row, TILE)] = block.T
+
+    crossing = {}
     for step in range(1, max(group.ahead for group in groups) + 1):
         for group, tile in order:
             if step <= group.ahead:
@@ -294,33 +332,12 @@
                     pass_on(group, tile, "down", step)
             if step == group.ahead:
                 rows = pl.ds(tile * TILE_ROWS, TILE_ROWS)
-                crossing.append(copies.start(out_ref.at[core, rows, :], out_ref.at[core, rows, :], place.partner()))
-    for copy in crossing:
+                crossing[tile] = copies.start(tiles_ref.at[core, rows, :], tiles_ref.at[core, rows, :],
+                                              place.partner())
+                unpack(core, tile)
+    for tile, copy in crossing.items():
         copy.wait_recv()
-    copies.drain()
-
-
-def gram_everywhere(field_rows, chips):
-    groups = [Group(chips, axes, tiles) for axes, tiles in GROUPS]
-    depth, order = field_rows.shape
-    count = 1 + len(TILES[0]) + sum(group.copies() for group in groups)
-    return pl.pallas_call(
-        functools.partial(gram_kernel, chips),
-        out_shape=jax.ShapeDtypeStruct((CORES, HALF_ROWS, LANES), jnp.float32),
-        in_specs=[VMEM],
-        out_specs=VMEM,
-        scratch_shapes=[pltpu.VMEM((CORES * depth, order), jnp.float32), pltpu.VMEM((HALF_ROWS, LANES), jnp.float32)]
-        + [shape for group in groups for shape in group.scratch()]
-        + [pltpu.SemaphoreType.DMA((count,)), pltpu.SemaphoreType.DMA((count,))],
-        compiler_params=pltpu.CompilerParams(collective_id=0, has_side_effects=True, vmem_limit_bytes=48 << 20),
-    )(field_rows)
-
-
-def mode_two_kernel(chips, core_ref, out_ref, leaving, cells, split, terms, rows_y, rows_x, send_sem, recv_sem):
-    place, copies = Place(chips), Copies(send_sem, recv_sem)
-    devices = CORES * chips["z"]
-    others = [(place.narrow + offset) % devices for offset in range(1, devices)]
-    greet([(narrow, place.wide) for narrow in others] + place.along("y") + place.along("x"))
+        unpack(1 - core, tile)
 
     def regroup(source, target):
         target[place.narrow] = source[place.narrow]
@@ -333,55 +350,8 @@
             copy.wait_recv()
         return functools.reduce(lambda total, slot: total + slots[slot], range(1, chips[axis]), slots[0])
 
-    for index in range(devices):
-        leaving[index] = core_ref[pl.ds(index, ROWS, stride=devices), :]
-    for copy in regroup(leaving, cells):
-        copy.wait_recv()
-    block = cells[...].reshape(devices * ROWS, RANK)
-    split[...] = product_of_rows(block, block).reshape(devices, ROWS, devices * ROWS)
-    for copy in regroup(split, terms):
-        copy.wait_recv()
-    total = functools.reduce(lambda total, slot: total + terms[slot], range(1, devices), terms[0])
-    total = sum_along("y", rows_y, total)
-    out_ref[...] = sum_along("x", rows_x, total)
-    copies.drain()
-
-
-def mode_two_rows(core_cells, chips):
-    devices = CORES * chips["z"]
-    width = devices * ROWS
-    count = 2 * (devices - 1) + chips["y"] + chips["x"] - 2
-
-    def tiles(number, lanes):
-        return pltpu.VMEM((number, ROWS, lanes), jnp.float32)
-
-    return pl.pallas_call(
-        functools.partial(mode_two_kernel, chips),
-        out_shape=jax.ShapeDtypeStruct((ROWS, width), jnp.float32),
-        in_specs=[VMEM],
-        out_specs=VMEM,
-        scratch_shapes=[tiles(devices, RANK), tiles(devices, RANK), tiles(devices, width), tiles(devices, width),
-                        tiles(chips["y"], width), tiles(chips["x"], width),
-                        pltpu.SemaphoreType.DMA((count,)), pltpu.SemaphoreType.DMA((count,))],
-        compiler_params=pltpu.CompilerParams(collective_id=1, has_side_effects=True),
-    )(core_cells)
-
-
-def orthonormal_kernel(rows_ref, out_ref):
-    rows = rows_ref[...]
-    out_ref[...] = product(inverse_factor(product_of_rows(rows, rows)), rows)
-
-
-def iteration_kernel(tiles_ref, rows_ref, field_ref, core_ref, gram, current):
-    for side in range(CORES):
-        for number, (row, column) in enumerate(TILES[side]):
-            start = number * TILE_ROWS
-            tile = jnp.concatenate([tiles_ref[side, start:start + TILE, :],
-                                    tiles_ref[side, start + TILE:start + 2 * TILE, :]], axis=1)
-            gram[row * TILE:(row + 1) * TILE, column * TILE:(column + 1) * TILE] = tile
-            if row != column:
-                gram[column * TILE:(column + 1) * TILE, row * TILE:(row + 1) * TILE] = tile.T
-    current[...] = product(rows_ref[...], gram[...])
+    arriving = regroup(leaving, cells)
+    current[...] = product(current[...], gram[...])
 
     def sweep(index, carry):
         rows = current[...]
@@ -392,34 +362,52 @@
     lax.fori_loop(0, ITERS - 1, sweep, 0)
     rows = current[...]
     subspace = product(inverse_factor(product_of_rows(rows, rows)), rows)
-    core_ref[...] = product_of_rows(field_ref[...], subspace)
+    for copy in arriving:
+        copy.wait_recv()
+    block = product_of_rows(cells[...].reshape(devices * ROWS, cells.shape[2]), subspace)
+    split[...] = product_of_rows(block, block).reshape(devices, ROWS, devices * ROWS)
+    for copy in regroup(split, terms):
+        copy.wait_recv()
+    total = functools.reduce(lambda total, slot: total + terms[slot], range(1, devices), terms[0])
+    out_ref[...] = sum_along("x", rows_x, sum_along("y", rows_y, total))
+    copies.drain()
 
 
 VMEM = pl.BlockSpec(memory_space=pltpu.VMEM)
+
+
+def mode_two_rows(field_rows, start_block, chips):
+    groups = [Group(chips, axes, tiles) for axes, tiles in GROUPS]
+    depth, order = field_rows.shape
+    devices = CORES * chips["z"]
+    width = devices * ROWS
+    count = (1 + len(TILES[0]) + sum(group.copies() for group in groups) + 2 * (devices - 1) + chips["y"] + chips["x"]
+             - 2)
+
+    def floats(*shape):
+        return pltpu.VMEM(shape, jnp.float32)
+
+    return pl.pallas_call(
+        functools.partial(hosvd_kernel, chips),
+        out_shape=jax.ShapeDtypeStruct((ROWS, width), jnp.float32),
+        in_specs=[VMEM, VMEM],
+        out_specs=VMEM,
+        scratch_shapes=[floats(CORES * depth, order), floats(HALF_ROWS, LANES), floats(CORES, HALF_ROWS, LANES),
+                        floats(order, order), floats(RANK, order), floats(devices, ROWS, order),
+                        floats(devices, ROWS, order), floats(devices, ROWS, width), floats(devices, ROWS, width),
+                        floats(chips["y"], ROWS, width), floats(chips["x"], ROWS, width)]
+        + [shape for group in groups for shape in group.scratch()]
+        + [pltpu.SemaphoreType.DMA((count,)), pltpu.SemaphoreType.DMA((count,))],
+        compiler_params=pltpu.CompilerParams(collective_id=0, has_side_effects=True, vmem_limit_bytes=48 << 20),
+    )(field_rows, start_block)
 
 
 def shards(chips, field, start_block):
     cells_two, cells_three, order_one = field.shape
-    unfolded = field.reshape(cells_two * cells_three, order_one)
-    start_rows = pl.pallas_call(
-        orthonormal_kernel,
-        out_shape=jax.ShapeDtypeStruct((RANK, order_one), jnp.float32),
-        in_specs=[VMEM],
-        out_specs=VMEM,
-    )(start_block.T)
-    gram_tiles = gram_everywhere(unfolded, chips)
-    core_cells = pl.pallas_call(
-        iteration_kernel,
-        out_shape=jax.ShapeDtypeStruct((cells_two * cells_three, RANK), jnp.float32),
-        in_specs=[VMEM, VMEM, VMEM],
-        out_specs=VMEM,
-        scratch_shapes=[pltpu.VMEM((order_one, order_one), jnp.float32), pltpu.VMEM((RANK, order_one), jnp.float32)],
-        compiler_params=pltpu.CompilerParams(vmem_limit_bytes=48 << 20),
-    )(gram_tiles, start_rows, unfolded)
-    rows = mode_two_rows(core_cells, chips)
+    rows = mode_two_rows(field.reshape(cells_two * cells_three, order_one), start_block, chips)
     columns = rows.shape[1] // lax.axis_size("wide")
     finished = lax.dynamic_slice_in_dim(rows, lax.axis_index("wide") * columns, columns, axis=1)
-    return finished / (RANK * B3 * lax.axis_size("wide"))
+    return finished / (RANK * cells_three * lax.axis_size("wide"))
 
 
 def solution(mesh, chips_y=CHIPS_Y):

time: 132 us -> 110 us (0.83)
  Pallas kernels: 126 us -> 107 us
  local copies, waits for them, and re-layouts: 4.35 us -> 2.74 us
    pallas_call x4 -> x1, Pallas kernels: 126 us -> 107 us  [mode_two_rows(): pl.pallas_call(functools.partial(hosvd_kernel, chips), out_shape=jax.Shap...]
    unnamed x7 -> x4, local copies, waits for them, and re-layouts: 3.7 us -> 2.08 us
where the time goes in v3:
time: 110 us
  Pallas kernels  107 us (97%)
  local copies, waits for them, and re-layouts  2.74 us (2%)
    pallas_call x1, Pallas kernels, mode_two_rows(): pl.pallas_call(functools.partial(hosvd_kernel, chips), out_shape=jax.Shap...  107 us

profile of v3, /device:TPU:6, one launch (start us, length us, event | category | flops | bytes accessed | tf_op | source)
XLA Modules:
  0.0 110.2 jit_solution(6931253645228398920)
XLA Ops:
  0.0 0.0 copy-start
  0.0 1.0 copy-done
  1.0 0.0 copy-start.1
  1.0 1.0 copy-done.1
  2.1 107.4 %shard_map.28 = f32[8,128]{1,0:T(8,128)S(1)} custom-call(f32[128,1024]{1,0:T(8,128)S(1)} %bitcast.1, f32[1024,128]{1,0:T(8,128)S(1)} %copy-done.1), custom_call_target="tpu_custom_call" | custom-call | tf_op jit(solution)/shard_map/pallas_call | solution.py:390
  109.5 0.1 dynamic-slice_multiply_fusion
  109.5 0.7 copy.3
Async XLA Ops:
  0.0 1.0 copy-start
  1.0 1.0 copy-start.1

commit v4 on v3

--- a/solution.py
+++ b/solution.py
@@ -97,9 +97,13 @@
                            preferred_element_type=jnp.float32)
 
 
-def product_of_columns(left, right):
-    return lax.dot_general(left.T, right, (((1,), (0,)), ((), ())), precision=HIGHEST,
-                           preferred_element_type=jnp.float32)
+def two_terms(values):
+    high = values.astype(jnp.bfloat16)
+    return high, (values - high.astype(jnp.float32)).astype(jnp.bfloat16)
+
+
+def term_product(left, right, contract):
+    return lax.dot_general(left, right, ((contract, (0,)), ((), ())), preferred_element_type=jnp.float32)
 
 
 class Place:
@@ -169,7 +173,7 @@
 
     def copies(self):
         links = len(self.tiles) * (self.ring - 1)
-        return 2 * links + 2 * (self.chips[self.second] - 1) + self.chips[self.third] - 1
+        return 2 * links + len(self.tiles) * self.ring + 2 * (self.chips[self.second] - 1) + self.chips[self.third] - 1
 
     def take(self, refs):
         self.up, self.down, self.sums, self.parts, self.slots, self.gathered = refs
@@ -183,8 +187,8 @@
     rows_ref[...] = product(factor, rows_ref[...])
 
 
-def hosvd_kernel(chips, field_ref, start_ref, out_ref, joined, mine, tiles_ref, gram, current, leaving, cells, split,
-                 terms, rows_y, rows_x, *rest):
+def hosvd_kernel(chips, field_hbm, start_hbm, out_ref, start_ref, joined, joined_terms, mine, tiles_ref, gram, current,
+                 ahead, leaving, cells, split, terms, rows_y, rows_x, load_sem, *rest):
     groups = [Group(chips, axes, tiles) for axes, tiles in GROUPS]
     for number, group in enumerate(groups):
         group.take(rest[6 * number:6 * number + 6])
@@ -198,14 +202,19 @@
     greeted = [(narrow, place.wide) for narrow in others] + place.along("y") + place.along("x")
     for device in greeted:
         pl.semaphore_signal(barrier, inc=1, device_id=device, device_id_type=MESH_ID)
+    depth, order_one = field_hbm.shape
+    own = aligned(core * depth, depth)
+    loads = [pltpu.make_async_copy(field_hbm, joined.at[own, :], load_sem.at[0]),
+             pltpu.make_async_copy(start_hbm, start_ref, load_sem.at[1])]
+    for load in loads:
+        load.start()
+    loads[0].wait()
+    leaving[...] = jnp.swapaxes(joined[own, :].reshape(ROWS, devices, order_one), 0, 1)
+    pl.semaphore_wait(barrier, len(greeted))
+
+    exchange = copies.start(joined.at[own, :], joined.at[own, :], place.partner())
+    loads[1].wait()
     current[...] = start_ref[...].T
-    leaving[...] = jnp.swapaxes(field_ref[...].reshape(ROWS, devices, field_ref.shape[1]), 0, 1)
-    pl.semaphore_wait(barrier, len(greeted))
-
-    depth = field_ref.shape[0]
-    own = aligned(core * depth, depth)
-    exchange = copies.start(field_ref, joined.at[own, :], place.partner())
-    joined[own, :] = field_ref[...]
     starting = start_rows(current)
 
     def advance(panels):
@@ -214,6 +223,8 @@
 
     advance(1)
     exchange.wait_recv()
+    for number, term in enumerate(two_terms(joined[...])):
+        joined_terms[number] = term
 
     moving = {}
 
@@ -229,8 +240,11 @@
     for group, tile in order:
         rows, columns = (TILES[0][tile][side] + core * (TILES[1][tile][side] - TILES[0][tile][side])
                          for side in range(2))
-        block = product_of_columns(joined[:, pl.ds(pl.multiple_of(rows * TILE, TILE), TILE)],
-                                   joined[:, pl.ds(pl.multiple_of(columns * TILE, TILE), TILE)])
+        row_high, row_low, column_high, column_low = (
+            joined_terms[number, :, pl.ds(pl.multiple_of(side * TILE, TILE), TILE)]
+            for side in (rows, columns) for number in range(2))
+        block = term_product(row_high, column_high, (0,)) + (
+            term_product(row_high, column_low, (0,)) + term_product(row_low, column_high, (0,)))
         for half in range(TILE // LANES):
             start = tile * TILE_ROWS + half * TILE
             mine[start:start + TILE, :] = block[:, half * LANES:(half + 1) * LANES]
@@ -240,7 +254,7 @@
 
     pieces = {}
     for step in range(1, max(group.ahead for group in groups) + 1):
-        advance(2)
+        advance(3)
         for group, tile in order:
             index = group.tiles.index(tile)
             if step < group.ahead:
@@ -280,7 +294,7 @@
         group.slots[here] = total
         pieces[group] = [copies.start(group.slots.at[here], group.slots.at[here], device)
                          for device in place.along(group.third)]
-    advance(3)
+    advance(RANK)
     for group in arrival:
         for copy in pieces[group]:
             copy.wait_recv()
@@ -292,13 +306,21 @@
         pieces[group] = [copies.start(group.gathered.at[here], group.gathered.at[here], device)
                          for device in place.along(group.second)]
 
+    crossing = {tile: [] for group in groups for tile in group.tiles}
+
+    def cross(tile, rows):
+        crossing[tile].append(copies.start(tiles_ref.at[core, rows, :], tiles_ref.at[core, rows, :], place.partner()))
+
     def pass_on(group, tile, way, step):
         sign = 1 if way == "up" else -1
         rows = group.rows_of(tile, place.step(group.first, -sign * step))
+        if way == "up" or step:
+            cross(tile, rows)
+        if step == (group.ahead if way == "up" else group.behind):
+            return
         device = place.device(group.first, place.step(group.first, sign))
         moving[tile, way, step] = copies.start(tiles_ref.at[core, rows, :], tiles_ref.at[core, rows, :], device)
 
-    advance(RANK)
     for group in arrival:
         for copy in pieces[group]:
             copy.wait_recv()
@@ -316,28 +338,32 @@
         start = tile * TILE_ROWS
         block = jnp.concatenate([tiles_ref[side, start:start + TILE, :],
                                  tiles_ref[side, start + TILE:start + 2 * TILE, :]], axis=1)
-        gram[pl.ds(row, TILE), pl.ds(column, TILE)] = block
-        gram[pl.ds(column, TILE), pl.ds(row, TILE)] = block.T
-
-    crossing = {}
+        for number, term in enumerate(two_terms(block)):
+            gram[number, pl.ds(row, TILE), pl.ds(column, TILE)] = term
+        for number, term in enumerate(two_terms(block.T)):
+            gram[number, pl.ds(column, TILE), pl.ds(row, TILE)] = term
+
+    def unpack_across(tile):
+        for copy in crossing[tile]:
+            copy.wait_recv()
+        unpack(1 - core, tile)
+
+    waiting = []
     for step in range(1, max(group.ahead for group in groups) + 1):
         for group, tile in order:
             if step <= group.ahead:
                 moving[tile, "up", step - 1].wait_recv()
-                if step < group.ahead:
-                    pass_on(group, tile, "up", step)
+                pass_on(group, tile, "up", step)
             if step <= group.behind:
                 moving[tile, "down", step - 1].wait_recv()
-                if step < group.behind:
-                    pass_on(group, tile, "down", step)
-            if step == group.ahead:
-                rows = pl.ds(tile * TILE_ROWS, TILE_ROWS)
-                crossing[tile] = copies.start(tiles_ref.at[core, rows, :], tiles_ref.at[core, rows, :],
-                                              place.partner())
-                unpack(core, tile)
-    for tile, copy in crossing.items():
-        copy.wait_recv()
-        unpack(1 - core, tile)
+                pass_on(group, tile, "down", step)
+        for tile in waiting:
+            unpack_across(tile)
+        waiting = [tile for group, tile in order if step == group.ahead]
+        for tile in waiting:
+            unpack(core, tile)
+    for tile in waiting:
+        unpack_across(tile)
 
     def regroup(source, target):
         target[place.narrow] = source[place.narrow]
@@ -351,20 +377,28 @@
         return functools.reduce(lambda total, slot: total + slots[slot], range(1, chips[axis]), slots[0])
 
     arriving = regroup(leaving, cells)
-    current[...] = product(current[...], gram[...])
+
+    def gram_times(rows):
+        high, low = two_terms(rows)
+        both = term_product(jnp.concatenate([high, low], axis=0), gram[0], (1,))
+        ahead[...] = both[:RANK] + (both[RANK:] + term_product(high, gram[1], (1,)))
+
+    gram_times(current[...])
+    current[...] = ahead[...]
 
     def sweep(index, carry):
         rows = current[...]
         factor = inverse_factor(product_of_rows(rows, rows))
-        current[...] = product(factor, product(rows, gram[...]))
+        gram_times(rows)
+        current[...] = product(factor, ahead[...])
         return carry
 
     lax.fori_loop(0, ITERS - 1, sweep, 0)
     rows = current[...]
-    subspace = product(inverse_factor(product_of_rows(rows, rows)), rows)
     for copy in arriving:
         copy.wait_recv()
-    block = product_of_rows(cells[...].reshape(devices * ROWS, cells.shape[2]), subspace)
+    core_rows = product_of_rows(cells[...].reshape(devices * ROWS, order_one), rows)
+    block = product_of_rows(core_rows, inverse_factor(product_of_rows(rows, rows)))
     split[...] = product_of_rows(block, block).reshape(devices, ROWS, devices * ROWS)
     for copy in regroup(split, terms):
         copy.wait_recv()
@@ -387,15 +421,20 @@
     def floats(*shape):
         return pltpu.VMEM(shape, jnp.float32)
 
+    def terms(*shape):
+        return pltpu.VMEM((2, *shape), jnp.bfloat16)
+
     return pl.pallas_call(
         functools.partial(hosvd_kernel, chips),
         out_shape=jax.ShapeDtypeStruct((ROWS, width), jnp.float32),
-        in_specs=[VMEM, VMEM],
+        in_specs=[pl.BlockSpec(memory_space=pl.ANY)] * 2,
         out_specs=VMEM,
-        scratch_shapes=[floats(CORES * depth, order), floats(HALF_ROWS, LANES), floats(CORES, HALF_ROWS, LANES),
-                        floats(order, order), floats(RANK, order), floats(devices, ROWS, order),
+        scratch_shapes=[floats(order, RANK), floats(CORES * depth, order), terms(CORES * depth, order),
+                        floats(HALF_ROWS, LANES), floats(CORES, HALF_ROWS, LANES), terms(order, order),
+                        floats(RANK, order), floats(RANK, order), floats(devices, ROWS, order),
                         floats(devices, ROWS, order), floats(devices, ROWS, width), floats(devices, ROWS, width),
-                        floats(chips["y"], ROWS, width), floats(chips["x"], ROWS, width)]
+                        floats(chips["y"], ROWS, width), floats(chips["x"], ROWS, width),
+                        pltpu.SemaphoreType.DMA((2,))]
         + [shape for group in groups for shape in group.scratch()]
         + [pltpu.SemaphoreType.DMA((count,)), pltpu.SemaphoreType.DMA((count,))],
         compiler_params=pltpu.CompilerParams(collective_id=0, has_side_effects=True, vmem_limit_bytes=48 << 20),

time: 110 us -> 106 us (0.964)
  Pallas kernels: 107 us -> 102 us
    pallas_call x1, Pallas kernels: 107 us -> 102 us  [mode_two_rows(): pl.pallas_call(functools.partial(hosvd_kernel, chips), out_shape=jax.Shap...]
where the time goes in v4:
time: 106 us; the launch traced here: 105 us
  Pallas kernels  102 us (96%)
  local copies, waits for them, and re-layouts  2.74 us (3%)
    pallas_call x1, Pallas kernels, mode_two_rows(): pl.pallas_call(functools.partial(hosvd_kernel, chips), out_shape=jax.Shap...  102 us

profile of v4, /device:TPU:6, one launch (start us, length us, event | category | flops | bytes accessed | tf_op | source)
XLA Modules:
  0.0 105.1 jit_solution(12096153044930985180)
XLA Ops:
  0.0 0.0 copy-start
  0.0 1.0 copy-done
  1.0 0.0 copy-start.1
  1.0 1.0 copy-done.1
  2.1 102.3 %shard_map.28 = f32[8,128]{1,0:T(8,128)S(1)} custom-call(f32[128,1024]{1,0:T(8,128)S(1)} %bitcast.1, f32[1024,128]{1,0:T(8,128)S(1)} %copy-done.1), custom_call_target="tpu_custom_call" | custom-call | tf_op jit(solution)/shard_map/pallas_call | solution.py:427
  104.4 0.1 dynamic-slice_multiply_fusion
  104.5 0.7 copy.3
Async XLA Ops:
  0.0 1.0 copy-start
  1.0 1.0 copy-start.1

commit v5 on v4

--- a/solution.py
+++ b/solution.py
@@ -157,6 +157,7 @@
         self.tiles = tiles
         self.ring = chips[self.first]
         self.ahead, self.behind = self.ring // 2, (self.ring - 1) // 2
+        self.relayed = self.ring == 8
         self.block = TILE_ROWS // self.ring
         self.piece = self.block // chips[self.second]
         self.rows = self.piece * len(tiles)
@@ -236,7 +237,39 @@
         device = place.device(group.first, place.step(group.first, -1))
         moving[tile, "down", step] = copies.start(source, group.down.at[group.tiles.index(tile), step], device)
 
-    order = [(group, group.tiles[turn]) for turn in range(2) for group in groups if turn < len(group.tiles)]
+    def own_block(group, tile, offset):
+        return group.rows_of(tile, place.step(group.first, offset))
+
+    def put(group, tile, name, source, target, offset):
+        device = place.device(group.first, place.step(group.first, offset))
+        moving[tile, name] = copies.start(source, target, device)
+
+    def spread(group, tile):
+        index = group.tiles.index(tile)
+        for name, target, to, via in (("far", group.up.at[index, 0], -4, -2), ("mid", group.up.at[index, 1], -3, -1),
+                                      ("back", group.down.at[index, 0], 3, 1), ("left", group.up.at[index, 2], -1, -1),
+                                      ("right", group.down.at[index, 1], 1, 1)):
+            put(group, tile, name, mine.at[own_block(group, tile, to), :], target, via)
+
+    def collect(group, tile):
+        index = group.tiles.index(tile)
+        moving[tile, "far"].wait_recv()
+        moving[tile, "mid"].wait_recv()
+        group.up[index, 0] = group.up[index, 0] + group.up[index, 1] + mine[own_block(group, tile, -2), :]
+        put(group, tile, "up", group.up.at[index, 0], group.up.at[index, 3], -2)
+        moving[tile, "back"].wait_recv()
+        group.down[index, 0] = group.down[index, 0] + mine[own_block(group, tile, 2), :]
+        put(group, tile, "down", group.down.at[index, 0], group.down.at[index, 2], 2)
+
+    def collected(group, tile):
+        index = group.tiles.index(tile)
+        for name in ("left", "right", "up", "down"):
+            moving[tile, name].wait_recv()
+        return (mine[own_block(group, tile, 0), :] + group.up[index, 2] + group.down[index, 1] + group.up[index, 3]
+                + group.down[index, 2])
+
+    order = [(group, group.tiles[turn]) for turn in range(2) for group in groups if len(group.tiles) == 2]
+    order += [(group, tile) for group in groups for tile in group.tiles if len(group.tiles) == 1]
     for group, tile in order:
         rows, columns = (TILES[0][tile][side] + core * (TILES[1][tile][side] - TILES[0][tile][side])
                          for side in range(2))
@@ -248,14 +281,33 @@
         for half in range(TILE // LANES):
             start = tile * TILE_ROWS + half * TILE
             mine[start:start + TILE, :] = block[:, half * LANES:(half + 1) * LANES]
+        if group.relayed:
+            spread(group, tile)
+            continue
         send_ahead(group, tile, mine.at[group.rows_of(tile, place.step(group.first, group.ahead)), :], 0)
         if group.behind:
             send_behind(group, tile, mine.at[group.rows_of(tile, place.step(group.first, -group.behind)), :], 0)
 
-    pieces = {}
-    for step in range(1, max(group.ahead for group in groups) + 1):
-        advance(3)
-        for group, tile in order:
+    pieces = {group: [] for group in groups}
+
+    def keep(group, tile, total):
+        index = group.tiles.index(tile)
+        for part in range(chips[group.second]):
+            group.sums[part, index * group.piece:(index + 1) * group.piece, :] = (
+                total[part * group.piece:(part + 1) * group.piece, :])
+        if index == len(group.tiles) - 1:
+            for offset in range(1, chips[group.second]):
+                to = place.step(group.second, offset)
+                pieces[group].append(copies.start(group.sums.at[to], group.parts.at[offset - 1],
+                                                  place.device(group.second, to)))
+
+    relayed = [(group, tile) for group, tile in order if group.relayed]
+    ringed = [(group, tile) for group, tile in order if not group.relayed]
+    advance(6)
+    for group, tile in relayed:
+        collect(group, tile)
+    for step in range(1, max(group.ahead for group, _ in ringed) + 1):
+        for group, tile in ringed:
             index = group.tiles.index(tile)
             if step < group.ahead:
                 moving[tile, "up", step - 1].wait_recv()
@@ -273,15 +325,10 @@
                 if group.behind:
                     moving[tile, "down", group.behind - 1].wait_recv()
                     total = total + group.down[index, group.behind - 1]
-                for part in range(chips[group.second]):
-                    group.sums[part, index * group.piece:(index + 1) * group.piece, :] = (
-                        total[part * group.piece:(part + 1) * group.piece, :])
-                if index == len(group.tiles) - 1:
-                    pieces[group] = []
-                    for offset in range(1, chips[group.second]):
-                        to = place.step(group.second, offset)
-                        pieces[group].append(copies.start(group.sums.at[to], group.parts.at[offset - 1],
-                                                          place.device(group.second, to)))
+                keep(group, tile, total)
+    advance(6)
+    for group, tile in relayed:
+        keep(group, tile, collected(group, tile))
 
     arrival = sorted(groups, key=lambda group: group.ahead)
     advance(3)
@@ -321,6 +368,31 @@
         device = place.device(group.first, place.step(group.first, sign))
         moving[tile, way, step] = copies.start(tiles_ref.at[core, rows, :], tiles_ref.at[core, rows, :], device)
 
+    def hand(group, tile, name, block, offset):
+        rows = own_block(group, tile, block)
+        put(group, tile, name, tiles_ref.at[core, rows, :], tiles_ref.at[core, rows, :], offset)
+
+    def hand_out(group, tile):
+        for offset in (2, -2, 1, -1):
+            hand(group, tile, ("own", offset), 0, offset)
+        cross(tile, own_block(group, tile, 0))
+
+    def hand_on(group, tile):
+        moving[tile, ("own", 2)].wait_recv()
+        hand(group, tile, ("next", 2), -2, 2)
+        hand(group, tile, ("next", 1), -2, 1)
+        moving[tile, ("own", -2)].wait_recv()
+        hand(group, tile, ("next", -1), 2, -1)
+        moving[tile, ("own", 1)].wait_recv()
+        moving[tile, ("own", -1)].wait_recv()
+        for block in (-2, 2, -1, 1):
+            cross(tile, own_block(group, tile, block))
+
+    def handed(group, tile):
+        for offset, block in ((1, -3), (-1, 3), (2, -4)):
+            moving[tile, ("next", offset)].wait_recv()
+            cross(tile, own_block(group, tile, block))
+
     for group in arrival:
         for copy in pieces[group]:
             copy.wait_recv()
@@ -329,6 +401,9 @@
             for part in range(chips[group.second]):
                 tiles_ref[core, aligned(start + part * group.piece, group.piece), :] = (
                     group.gathered[part, index * group.piece:(index + 1) * group.piece, :])
+            if group.relayed:
+                hand_out(group, tile)
+                continue
             pass_on(group, tile, "up", 0)
             if group.behind:
                 pass_on(group, tile, "down", 0)
@@ -348,21 +423,25 @@
             copy.wait_recv()
         unpack(1 - core, tile)
 
-    waiting = []
-    for step in range(1, max(group.ahead for group in groups) + 1):
-        for group, tile in order:
+    for group, tile in relayed:
+        hand_on(group, tile)
+    for step in range(1, max(group.ahead for group, _ in ringed) + 1):
+        for group, tile in ringed:
             if step <= group.ahead:
                 moving[tile, "up", step - 1].wait_recv()
                 pass_on(group, tile, "up", step)
             if step <= group.behind:
                 moving[tile, "down", step - 1].wait_recv()
                 pass_on(group, tile, "down", step)
-        for tile in waiting:
-            unpack_across(tile)
-        waiting = [tile for group, tile in order if step == group.ahead]
-        for tile in waiting:
-            unpack(core, tile)
-    for tile in waiting:
+    for group, tile in ringed:
+        unpack(core, tile)
+    for group, tile in relayed:
+        handed(group, tile)
+    for group, tile in ringed:
+        unpack_across(tile)
+    for group, tile in relayed:
+        unpack(core, tile)
+    for group, tile in relayed:
         unpack_across(tile)
 
     def regroup(source, target):

time: 106 us -> 102 us (0.962)
  Pallas kernels: 102 us -> 98.8 us
    pallas_call x1, Pallas kernels: 102 us -> 98.8 us  [mode_two_rows(): pl.pallas_call(functools.partial(hosvd_kernel, chips), out_shape=jax.Shap...]
where the time goes in v5:
time: 102 us
  Pallas kernels  98.8 us (97%)
  local copies, waits for them, and re-layouts  2.74 us (3%)
    pallas_call x1, Pallas kernels, mode_two_rows(): pl.pallas_call(functools.partial(hosvd_kernel, chips), out_shape=jax.Shap...  98.8 us
    unnamed x4, local copies, waits for them, and re-layouts  2.08 us

profile of v5, /device:TPU:6, one launch (start us, length us, event | category | flops | bytes accessed | tf_op | source)
XLA Modules:
  0.0 101.6 jit_solution(12436755150082714889)
XLA Ops:
  0.0 0.0 copy-start
  0.0 1.0 %copy-done = f32[8,16,1024]{2,1,0:T(8,128)S(1)} copy-done((f32[8,16,1024]{2,1,0:T(8,128)S(1)}, f32[8,16,1024]{2,1,0:T(8,128)}, u32[]{:S(2)}) %copy-start) | copy-done | bytes 524312
  1.0 0.0 copy-start.1
  1.0 1.0 %copy-done.1 = f32[1024,128]{1,0:T(8,128)S(1)} copy-done((f32[1024,128]{1,0:T(8,128)S(1)}, f32[1024,128]{1,0:T(8,128)}, u32[]{:S(2)}) %copy-start.1) | copy-done | bytes 524312
  2.1 98.8 %shard_map.28 = f32[8,128]{1,0:T(8,128)S(1)} custom-call(f32[128,1024]{1,0:T(8,128)S(1)} %bitcast.1, f32[1024,128]{1,0:T(8,128)S(1)} %copy-done.1), custom_call_target="tpu_custom_call" | custom-call | tf_op jit(solution)/shard_map/pallas_call | solution.py:506
  100.9 0.1 dynamic-slice_multiply_fusion
  100.9 0.7 copy.3
Async XLA Ops:
  0.0 1.0 %copy-start = (f32[8,16,1024]{2,1,0:T(8,128)S(1)}, f32[8,16,1024]{2,1,0:T(8,128)}, u32[]{:S(2)}) copy-start(f32[8,16,1024]{2,1,0:T(8,128)} %param.2) | copy-start | bytes 1572868
  1.0 1.0 %copy-start.1 = (f32[1024,128]{1,0:T(8,128)S(1)}, f32[1024,128]{1,0:T(8,128)}, u32[]{:S(2)}) copy-start(f32[1024,128]{1,0:T(8,128)} %start_hbm.1) | copy-start | bytes 1572868
